TPU v7x, 32 devices: a whole 2x2x4 slice. The times are simulated.
32 devices in a mesh: node: 8 (over z, x), rep: 4 (over y, core).
Axes of the slice: x: 2, y: 2, z: 4, core: 2. Of those that a mesh axis runs over, the one named last changes fastest.
Arguments:
- features: bfloat16 [8192, 512], P(('node', 'rep')), may hold values from -6 to 6
- weight: bfloat16 [512, 512], replicated, may hold values from -0.25 to 0.25
- cotangent: bfloat16 [8192, 512], P(('node', 'rep')), may hold values from -6 to 6
- tile_values: bfloat16 [8192, 128, 128], P(('node', 'rep')), may hold values from -0.125 to 0.125
- tile_row: int32 [8192], P(('node', 'rep')), may hold values from 0 to 7
- tile_col: int32 [8192], P(('node', 'rep')), may hold values from 0 to 15
- tile_count: int32 [32], P(('node', 'rep')), may hold values from 64 to 256, as said below
Outputs:
- activation: bfloat16 [8192, 512], P(('node', 'rep'))
- weight_grad: float32 [512, 512], replicated
- feature_grad: bfloat16 [8192, 512], P(('node', 'rep'))
Inputs may be any that keep to these rules, and one draw needn't show every extreme that they name: `tile_count`: slots of a device below its count hold tiles, the others are ignored; some device uses all 256 slots.
All inputs are finite; a program needn't handle non-finite values.
Results may differ from a plain program's by a relative error of at most 0.023.
Values may be sent and summed in bfloat16 or wider, within the bound.
A program may use at most 128 MiB of HBM per device.

v0:
```python
import math
import jax
import jax.numpy as jnp
from jax import lax
from jax.sharding import PartitionSpec as P

TB = 128


def smooth_gate(values):
    return jax.nn.gelu(values, approximate=True)


def apply_tiles(
    tile_values, tile_row, tile_col, tile_count, sources, target_shape, backward, window_start
):
    group_size = min(32, tile_row.shape[0])
    filled = tile_count[0]
    turns_needed = (filled + group_size - 1) // group_size
    window_blocks = target_shape[0]

    def one_turn(turn_index, totals):
        offset = turn_index * group_size
        values = lax.dynamic_slice_in_dim(tile_values, offset, group_size, 0)
        rows_here = lax.dynamic_slice_in_dim(tile_row, offset, group_size, 0)
        cols_here = lax.dynamic_slice_in_dim(tile_col, offset, group_size, 0)
        slot_mask = (offset + jnp.arange(group_size, dtype=jnp.int32) < filled).astype(jnp.float32)
        if backward:
            local_cols = cols_here - window_start
            inside = ((local_cols >= 0) & (local_cols < window_blocks)).astype(jnp.float32)
            placed = jnp.clip(local_cols, 0, window_blocks - 1)
            product = jnp.einsum(
                "tji,tjf->tif", values, sources[rows_here], preferred_element_type=jnp.float32
            )
            return totals.at[placed].add(product * (slot_mask * inside)[:, None, None])
        product = jnp.einsum(
            "tij,tjf->tif", values, sources[cols_here], preferred_element_type=jnp.float32
        )
        return totals.at[rows_here].add(product * slot_mask[:, None, None])

    return lax.fori_loop(0, turns_needed, one_turn, jnp.zeros(target_shape, jnp.float32))


def local(features, weight, cotangent, tile_values, tile_row, tile_col, tile_count):
    rows_quarter = features.shape[0]
    feature_width = features.shape[1]
    rep_count = lax.axis_size("rep")
    node_count = lax.axis_size("node")
    scale = 1.0 / math.sqrt(rows_quarter * rep_count * node_count)
    gathered = lax.all_gather(features, "node", axis=0, tiled=True)
    source_blocks = gathered.reshape(-1, TB, feature_width)
    block_count = rows_quarter * rep_count // TB
    partial_value = apply_tiles(
        tile_values,
        tile_row,
        tile_col,
        tile_count,
        source_blocks,
        (block_count, TB, feature_width),
        False,
        0,
    ).reshape(block_count * TB, feature_width)
    aggregate_all = lax.psum(partial_value, "rep").astype(jnp.bfloat16)
    cotangent_all = lax.all_gather(cotangent, "rep", axis=0, tiled=True)
    pre = jnp.dot(aggregate_all, weight, preferred_element_type=jnp.float32)
    activated, pullback = jax.vjp(smooth_gate, pre)
    grad_all = pullback(cotangent_all.astype(jnp.float32))[0].astype(jnp.bfloat16)
    full_grad = jnp.dot(grad_all, weight.T, preferred_element_type=jnp.float32).astype(jnp.bfloat16)
    offset = lax.axis_index("rep") * rows_quarter
    own_aggregate = lax.dynamic_slice_in_dim(aggregate_all, offset, rows_quarter, 0)
    own_grad = lax.dynamic_slice_in_dim(grad_all, offset, rows_quarter, 0)
    weight_term = jnp.dot(own_aggregate.T, own_grad, preferred_element_type=jnp.float32)
    output_rows = lax.dynamic_slice_in_dim(activated, offset, rows_quarter, 0).astype(jnp.bfloat16)
    weight_grad = lax.psum(weight_term, ("node", "rep")) * scale
    grad_blocks = full_grad.reshape(block_count, TB, feature_width)
    contributions = apply_tiles(
        tile_values, tile_row, tile_col, tile_count, grad_blocks, source_blocks.shape, True, 0
    )
    feature_grad = lax.psum_scatter(
        contributions.reshape(-1, feature_width).astype(jnp.bfloat16),
        "node",
        scatter_dimension=0,
        tiled=True,
    )
    return (output_rows, weight_grad, feature_grad)


def solution(mesh):
    in_specs = (
        P(("node", "rep"), None),
        P(),
        P(("node", "rep"), None),
        P(("node", "rep"), None, None),
        P(("node", "rep")),
        P(("node", "rep")),
        P(("node", "rep")),
    )
    out_specs = (P(("node", "rep"), None), P(), P(("node", "rep"), None))
    return jax.shard_map(local, mesh=mesh, in_specs=in_specs, out_specs=out_specs, check_vma=False)
```

profile of v0, /device:TPU:0, one launch (start us, length us, event | category | flops | bytes accessed | tf_op | source)
XLA Modules:
  0.0 611.5 jit_solution(17007301135434615890)
XLA Ops:
  9.4 52.6 %all-gather.3.cloned.1.call-done = bf16[2048,512]{1,0:T(8,128)(2,1)} async-done(((bf16[256,512]{1,0:T(8,128)(2,1)}), bf16[2048,512]{1,0:T(8,128)(2,1)}) %all-gather.3.cloned.1.call-update) | async-done | bytes 2097168 | tf_op jit(solution)/shard_map/all_gather | solution.py:50
  62.3 95.9 %while.20 = (s32[]{:T(128)}, f32[8,128,512]{2,1,0:T(8,128)S(1)}, s32[]{:T(128)}, s32[256]{0:T(256)S(1)}, bf16[256,128,128]{2,1,0:T(8,128)(2,1)}, /*index=5*/s32[...) while((s32[]{:T(128)}, f32[8,128,512]{2,1,0:T(8,128)S(1)}, ...), condition=%wide.region_2.3_spmd, body=%wide.region_0.2_spmd.sunk | while | flops 541066560 | bytes 47191344 | solution.py:41
  63.0 4.4 gather_fusion
  67.4 7.2 %broadcast_multiply_fusion.5 = f32[32,128,512]{2,1,0:T(8,128)} fusion(f32[32]{0:T(128)S(1)} %compare_convert_fusion.3, bf16[32,128,512]{2,1,0:T(8,128)(2,1)} %gather_fusion, bf16[256,128,128]{2,1,0:T(8,128)(2,1)} %get-tuple-element.274, s32[]{:T(128)S(6)} %select_n.44), kind=kOutput, calls=%fused_computation.4.clone.1 | convolution fusion | flops 538968064 | bytes 13631620 | tf_op jit(solution)/shard_map/while/body/tij,tjf->tif/dot_general | solution.py:36
  74.6 11.8 %scatter_fusion = f32[8,128,512]{2,1,0:T(8,128)S(1)} fusion(f32[8,128,512]{2,1,0:T(8,128)S(1)} %get-tuple-element.259, s32[32]{0:T(128)S(1)} %get-tuple-element.234, f32[32,128,512]{2,1,0:T(8,128)} %broadcast_multiply_fusion.5), kind=kCustom, calls=%fused_computation.2.clone.1 | custom fusion | flops 2097152 | bytes 25165952 | tf_op jit(solution)/shard_map/while/body/scatter-add | solution.py:39
  87.2 4.4 gather_fusion
  91.5 7.0 %broadcast_multiply_fusion.5 = f32[32,128,512]{2,1,0:T(8,128)} fusion(f32[32]{0:T(128)S(1)} %compare_convert_fusion.3, bf16[32,128,512]{2,1,0:T(8,128)(2,1)} %gather_fusion, bf16[256,128,128]{2,1,0:T(8,128)(2,1)} %get-tuple-element.274, s32[]{:T(128)S(6)} %select_n.44), kind=kOutput, calls=%fused_computation.4.clone.1 | convolution fusion | flops 538968064 | bytes 13631620 | tf_op jit(solution)/shard_map/while/body/tij,tjf->tif/dot_general | solution.py:36
  98.5 11.8 %scatter_fusion = f32[8,128,512]{2,1,0:T(8,128)S(1)} fusion(f32[8,128,512]{2,1,0:T(8,128)S(1)} %get-tuple-element.259, s32[32]{0:T(128)S(1)} %get-tuple-element.234, f32[32,128,512]{2,1,0:T(8,128)} %broadcast_multiply_fusion.5), kind=kCustom, calls=%fused_computation.2.clone.1 | custom fusion | flops 2097152 | bytes 25165952 | tf_op jit(solution)/shard_map/while/body/scatter-add | solution.py:39
  111.1 4.4 gather_fusion
  115.4 7.0 %broadcast_multiply_fusion.5 = f32[32,128,512]{2,1,0:T(8,128)} fusion(f32[32]{0:T(128)S(1)} %compare_convert_fusion.3, bf16[32,128,512]{2,1,0:T(8,128)(2,1)} %gather_fusion, bf16[256,128,128]{2,1,0:T(8,128)(2,1)} %get-tuple-element.274, s32[]{:T(128)S(6)} %select_n.44), kind=kOutput, calls=%fused_computation.4.clone.1 | convolution fusion | flops 538968064 | bytes 13631620 | tf_op jit(solution)/shard_map/while/body/tij,tjf->tif/dot_general | solution.py:36
  122.4 11.7 %scatter_fusion = f32[8,128,512]{2,1,0:T(8,128)S(1)} fusion(f32[8,128,512]{2,1,0:T(8,128)S(1)} %get-tuple-element.259, s32[32]{0:T(128)S(1)} %get-tuple-element.234, f32[32,128,512]{2,1,0:T(8,128)} %broadcast_multiply_fusion.5), kind=kCustom, calls=%fused_computation.2.clone.1 | custom fusion | flops 2097152 | bytes 25165952 | tf_op jit(solution)/shard_map/while/body/scatter-add | solution.py:39
  134.9 4.4 gather_fusion
  139.3 7.0 %broadcast_multiply_fusion.5 = f32[32,128,512]{2,1,0:T(8,128)} fusion(f32[32]{0:T(128)S(1)} %compare_convert_fusion.3, bf16[32,128,512]{2,1,0:T(8,128)(2,1)} %gather_fusion, bf16[256,128,128]{2,1,0:T(8,128)(2,1)} %get-tuple-element.274, s32[]{:T(128)S(6)} %select_n.44), kind=kOutput, calls=%fused_computation.4.clone.1 | convolution fusion | flops 538968064 | bytes 13631620 | tf_op jit(solution)/shard_map/while/body/tij,tjf->tif/dot_general | solution.py:36
  146.3 11.8 %scatter_fusion = f32[8,128,512]{2,1,0:T(8,128)S(1)} fusion(f32[8,128,512]{2,1,0:T(8,128)S(1)} %get-tuple-element.259, s32[32]{0:T(128)S(1)} %get-tuple-element.234, f32[32,128,512]{2,1,0:T(8,128)} %broadcast_multiply_fusion.5), kind=kCustom, calls=%fused_computation.2.clone.1 | custom fusion | flops 2097152 | bytes 25165952 | tf_op jit(solution)/shard_map/while/body/scatter-add | solution.py:39
  158.1 87.7 %all-reduce.4 = bf16[1024,512]{1,0:T(8,128)(2,1)} all-reduce(f32[1024,512]{1,0:T(8,128)S(1)} %bitcast.16), channel_id=1, replica_groups=mesh['node'=8,'rep'=4] {'rep'}, use_global_device_ids=true, to_apply=%region_3.4 | all-reduce | flops 524288 | bytes 3145728 | tf_op jit(solution)/shard_map/psum | solution.py:63
  245.8 5.3 fusion.6
  256.8 117.3 %while.21 = (s32[]{:T(128)}, f32[16,128,512]{2,1,0:T(8,128)}, s32[]{:T(128)}, s32[256]{0:T(256)S(1)}, bf16[256,128,128]{2,1,0:T(8,128)(2,1)}, /*index=5*/s32[256...) while((s32[]{:T(128)}, f32[16,128,512]{2,1,0:T(8,128)}, ...), condition=%wide.region_7.8_spmd, body=%wide.region_5.7_spmd.sunk | while | flops 541066688 | bytes 47191480 | solution.py:41
  257.6 2.8 gather_fusion.1
  260.3 7.3 %broadcast_multiply_fusion.6 = f32[32,128,512]{2,1,0:T(8,128)} fusion(f32[32]{0:T(128)S(1)} %and_select_fusion.2, bf16[32,128,512]{2,1,0:T(8,128)(2,1)} %gather_fusion.1, bf16[256,128,128]{2,1,0:T(8,128)(2,1)} %get-tuple-element.310, s32[]{:T(128)S(6)} %select_n.46), kind=kOutput, calls=%fused_computation.11.clone.1 | convolution fusion | flops 538968064 | bytes 13631620 | tf_op jit(solution)/shard_map/while/body/tji,tjf->tif/dot_general | solution.py:32
  267.6 18.4 %scatter_fusion.1 = f32[16,128,512]{2,1,0:T(8,128)} fusion(f32[16,128,512]{2,1,0:T(8,128)} %get-tuple-element.295, s32[32]{0:T(128)S(1)} %get-tuple-element.244, f32[32,128,512]{2,1,0:T(8,128)} %broadcast_multiply_fusion.6), kind=kCustom, calls=%fused_computation.3.clone.1 | custom fusion | flops 2097152 | bytes 25165952 | tf_op jit(solution)/shard_map/while/body/scatter-add | solution.py:35
  286.8 2.8 gather_fusion.1
  289.5 7.3 %broadcast_multiply_fusion.6 = f32[32,128,512]{2,1,0:T(8,128)} fusion(f32[32]{0:T(128)S(1)} %and_select_fusion.2, bf16[32,128,512]{2,1,0:T(8,128)(2,1)} %gather_fusion.1, bf16[256,128,128]{2,1,0:T(8,128)(2,1)} %get-tuple-element.310, s32[]{:T(128)S(6)} %select_n.46), kind=kOutput, calls=%fused_computation.11.clone.1 | convolution fusion | flops 538968064 | bytes 13631620 | tf_op jit(solution)/shard_map/while/body/tji,tjf->tif/dot_general | solution.py:32
  296.8 18.7 %scatter_fusion.1 = f32[16,128,512]{2,1,0:T(8,128)} fusion(f32[16,128,512]{2,1,0:T(8,128)} %get-tuple-element.295, s32[32]{0:T(128)S(1)} %get-tuple-element.244, f32[32,128,512]{2,1,0:T(8,128)} %broadcast_multiply_fusion.6), kind=kCustom, calls=%fused_computation.3.clone.1 | custom fusion | flops 2097152 | bytes 25165952 | tf_op jit(solution)/shard_map/while/body/scatter-add | solution.py:35
  316.3 2.8 gather_fusion.1
  319.0 7.3 %broadcast_multiply_fusion.6 = f32[32,128,512]{2,1,0:T(8,128)} fusion(f32[32]{0:T(128)S(1)} %and_select_fusion.2, bf16[32,128,512]{2,1,0:T(8,128)(2,1)} %gather_fusion.1, bf16[256,128,128]{2,1,0:T(8,128)(2,1)} %get-tuple-element.310, s32[]{:T(128)S(6)} %select_n.46), kind=kOutput, calls=%fused_computation.11.clone.1 | convolution fusion | flops 538968064 | bytes 13631620 | tf_op jit(solution)/shard_map/while/body/tji,tjf->tif/dot_general | solution.py:32
  326.3 18.3 %scatter_fusion.1 = f32[16,128,512]{2,1,0:T(8,128)} fusion(f32[16,128,512]{2,1,0:T(8,128)} %get-tuple-element.295, s32[32]{0:T(128)S(1)} %get-tuple-element.244, f32[32,128,512]{2,1,0:T(8,128)} %broadcast_multiply_fusion.6), kind=kCustom, calls=%fused_computation.3.clone.1 | custom fusion | flops 2097152 | bytes 25165952 | tf_op jit(solution)/shard_map/while/body/scatter-add | solution.py:35
  345.5 2.8 gather_fusion.1
  348.2 7.3 %broadcast_multiply_fusion.6 = f32[32,128,512]{2,1,0:T(8,128)} fusion(f32[32]{0:T(128)S(1)} %and_select_fusion.2, bf16[32,128,512]{2,1,0:T(8,128)(2,1)} %gather_fusion.1, bf16[256,128,128]{2,1,0:T(8,128)(2,1)} %get-tuple-element.310, s32[]{:T(128)S(6)} %select_n.46), kind=kOutput, calls=%fused_computation.11.clone.1 | convolution fusion | flops 538968064 | bytes 13631620 | tf_op jit(solution)/shard_map/while/body/tji,tjf->tif/dot_general | solution.py:32
  355.5 18.5 %scatter_fusion.1 = f32[16,128,512]{2,1,0:T(8,128)} fusion(f32[16,128,512]{2,1,0:T(8,128)} %get-tuple-element.295, s32[32]{0:T(128)S(1)} %get-tuple-element.244, f32[32,128,512]{2,1,0:T(8,128)} %broadcast_multiply_fusion.6), kind=kCustom, calls=%fused_computation.3.clone.1 | custom fusion | flops 2097152 | bytes 25165952 | tf_op jit(solution)/shard_map/while/body/scatter-add | solution.py:35
  374.1 3.8 convert_element_type.37
  379.9 49.0 %all-reduce.3.cloned.1.call-done = f32[512,512]{1,0:T(8,128)} async-done(((f32[512,512]{1,0:T(8,128)}), f32[512,512]{1,0:T(8,128)}) %all-reduce.3.cloned.1.call-update) | async-done | bytes 1048592 | tf_op jit(solution)/shard_map/psum | solution.py:74
  431.2 173.9 %reduce-scatter.2.cloned.1.call-done = bf16[256,512]{1,0:T(8,128)(2,1)} async-done(((bf16[2048,512]{1,0:T(8,128)(2,1)}), bf16[256,512]{1,0:T(8,128)(2,1)}) %reduce-scatter.2.cloned.1.call-update) | async-done | bytes 262160 | tf_op jit(solution)/shard_map/reduce_scatter | solution.py:79
  (45 shorter events, 17.8 us)
Async XLA Ops:
  7.2 238.7 %copy-start = (bf16[512,512]{1,0:T(8,128)(2,1)S(1)}, bf16[512,512]{1,0:T(8,128)(2,1)}, u32[]{:S(2)}) copy-start(bf16[512,512]{1,0:T(8,128)(2,1)} %param.12) | copy-start | bytes 1572868
  7.2 55.1 %copy-start.1 = (s32[256]{0:T(256)S(1)}, s32[256]{0:T(256)}, u32[]{:S(2)}) copy-start(s32[256]{0:T(256)} %param.16) | copy-start | bytes 3076
  7.2 55.1 %copy-start.2 = (s32[256]{0:T(256)S(1)}, s32[256]{0:T(256)}, u32[]{:S(2)}) copy-start(s32[256]{0:T(256)} %param.15) | copy-start | bytes 3076
  7.2 54.8 %all-gather.3.cloned.1.call-start = ((), (), s32[]{:S(2)}) async-start(), calls=%async_computation.1 | async-start | bytes 2359296 | tf_op jit(solution)/shard_map/all_gather | solution.py:50
  7.9 237.9 %all-gather.5.cloned.1.call-start = ((), (), s32[]{:S(2)}) async-start(), calls=%async_computation.2 | async-start | bytes 1310720 | tf_op jit(solution)/shard_map/all_gather | solution.py:64
  8.7 420.2 %all-reduce.3.cloned.1.call-start = ((), (), s32[]{:S(2)}) async-start(), calls=%async_computation.3 | async-start | bytes 2097152 | tf_op jit(solution)/shard_map/psum | solution.py:74
  254.2 350.8 %reduce-scatter.2.cloned.1.call-start = ((), (), s32[]{:S(2)}) async-start(), calls=%async_computation.4 | async-start | bytes 2359296 | tf_op jit(solution)/shard_map/reduce_scatter | solution.py:79
Sparse Core Ops, SparseCore 0:
  10.1 51.7 all-gather.2
  63.5 15.2 all-gather.4
  254.3 174.4 all-reduce.2
  432.8 172.1 reduce-scatter.1
where the time goes:
time: 614 us; the launch traced here: 612 us
  waiting for transfers between devices  277 us (45%)
  other arithmetic  135 us (22%)
  blocking collectives  87.7 us (14%)
  matrix products  65.7 us (11%)
  local copies, waits for them, and re-layouts  31.2 us (5%)
  between operations  14.5 us (2%)
    reduce_scatter x1, waiting for transfers between devices, local(): lax.psum_scatter(contributions.reshape(-1, feature_width).astype(jnp.bflo...  174 us
    psum x1, blocking collectives, local(): aggregate_all = lax.psum(partial_value, 'rep').astype(jnp.bfloat16)  87.7 us
    scatter-add x4, other arithmetic, one_turn(): return totals.at[placed].add(product * (slot_mask * inside)[:, None, None])  73.9 us
    all_gather x1, waiting for transfers between devices, local(): gathered = lax.all_gather(features, 'node', axis=0, tiled=True)  52.6 us
    psum x1, waiting for transfers between devices, local(): weight_grad = lax.psum(weight_term, ('node', 'rep')) * scale  49 us
    scatter-add x4, other arithmetic, one_turn(): return totals.at[rows_here].add(product * slot_mask[:, None, None])  47.1 us
    dot_general x4, matrix products, one_turn(): jnp.einsum('tji,tjf->tif', values, sources[rows_here], preferred_element_...  29.1 us
    dot_general x4, matrix products, one_turn(): jnp.einsum('tij,tjf->tif', values, sources[cols_here], preferred_element_...  28.2 us
  transfers between devices with their start and end apart: 4, of which 3 were waited for; matrix products, arithmetic and copies ran while one was open for 37% of the time, Pallas kernels for 0%

commit v1 on v0

--- a/solution.py
+++ b/solution.py
@@ -1,3 +1,4 @@
+import functools
 import math
 import jax
 import jax.numpy as jnp
@@ -5,6 +6,15 @@
 from jax.sharding import PartitionSpec as P
 
 TB = 128
+
+
+def list_panel(frame_in, axis_tag, link_axis):
+    for ix in (link_axis, axis_tag):
+        frame_in = lax.psum(frame_in, ix)
+    return frame_in
+
+
+connect_sides = functools.partial(list_panel, axis_tag="node", link_axis="rep")
 
 
 def smooth_gate(values):
@@ -71,7 +81,7 @@
     own_grad = lax.dynamic_slice_in_dim(grad_all, offset, rows_quarter, 0)
     weight_term = jnp.dot(own_aggregate.T, own_grad, preferred_element_type=jnp.float32)
     output_rows = lax.dynamic_slice_in_dim(activated, offset, rows_quarter, 0).astype(jnp.bfloat16)
-    weight_grad = lax.psum(weight_term, ("node", "rep")) * scale
+    weight_grad = connect_sides(weight_term) * scale
     grad_blocks = full_grad.reshape(block_count, TB, feature_width)
     contributions = apply_tiles(
         tile_values, tile_row, tile_col, tile_count, grad_blocks, source_blocks.shape, True, 0

time: 614 us -> 647 us (1.054)
  waiting for transfers between devices: 277 us -> 310 us
    psum x1 -> x2, waiting for transfers between devices: 49 us -> 79.5 us  [list_panel(): frame_in = lax.psum(frame_in, ix)]
  transfers between devices with their start and end apart: 4 -> 5, of which waited for: 3 -> 3; matrix products, arithmetic and copies ran while one was open for 37% -> 35% of each run, Pallas kernels for 0% -> 0%
where the time goes in v1:
time: 647 us; the launch traced here: 645 us
  waiting for transfers between devices  310 us (48%)
  other arithmetic  135 us (21%)
  blocking collectives  87.7 us (14%)
  matrix products  65.7 us (10%)
  local copies, waits for them, and re-layouts  31.3 us (5%)
  between operations  14.5 us (2%)
    reduce_scatter x1, waiting for transfers between devices, local(): lax.psum_scatter(contributions.reshape(-1, feature_width).astype(jnp.bflo...  176 us
    psum x1, blocking collectives, local(): aggregate_all = lax.psum(partial_value, 'rep').astype(jnp.bfloat16)  87.7 us
    psum x2, waiting for transfers between devices, list_panel(): frame_in = lax.psum(frame_in, ix)  79.5 us
    scatter-add x4, other arithmetic, one_turn(): return totals.at[placed].add(product * (slot_mask * inside)[:, None, None])  73.8 us
    all_gather x1, waiting for transfers between devices, local(): gathered = lax.all_gather(features, 'node', axis=0, tiled=True)  52.6 us
    scatter-add x4, other arithmetic, one_turn(): return totals.at[rows_here].add(product * slot_mask[:, None, None])  47.1 us
    dot_general x4, matrix products, one_turn(): jnp.einsum('tji,tjf->tif', values, sources[rows_here], preferred_element_...  29.2 us
    dot_general x4, matrix products, one_turn(): jnp.einsum('tij,tjf->tif', values, sources[cols_here], preferred_element_...  28.2 us
  transfers between devices with their start and end apart: 5, of which 3 were waited for; matrix products, arithmetic and copies ran while one was open for 35% of the time, Pallas kernels for 0%

profile of v1, /device:TPU:0, one launch (start us, length us, event | category | flops | bytes accessed | tf_op | source)
XLA Modules:
  0.0 644.5 jit_solution(5589147025536534071)
XLA Ops:
  9.4 52.6 %all-gather.3.cloned.1.call-done = bf16[2048,512]{1,0:T(8,128)(2,1)} async-done(((bf16[256,512]{1,0:T(8,128)(2,1)}), bf16[2048,512]{1,0:T(8,128)(2,1)}) %all-gather.3.cloned.1.call-update) | async-done | bytes 2097168 | tf_op jit(solution)/shard_map/all_gather | solution.py:60
  62.3 95.9 %while.20 = (s32[]{:T(128)}, f32[8,128,512]{2,1,0:T(8,128)S(1)}, s32[]{:T(128)}, s32[256]{0:T(256)S(1)}, bf16[256,128,128]{2,1,0:T(8,128)(2,1)}, /*index=5*/s32[...) while((s32[]{:T(128)}, f32[8,128,512]{2,1,0:T(8,128)S(1)}, ...), condition=%wide.region_2.3_spmd, body=%wide.region_0.2_spmd.sunk | while | flops 541066560 | bytes 47191344 | solution.py:51
  63.0 4.4 gather_fusion
  67.4 7.2 %broadcast_multiply_fusion.5 = f32[32,128,512]{2,1,0:T(8,128)} fusion(f32[32]{0:T(128)S(1)} %compare_convert_fusion.3, bf16[32,128,512]{2,1,0:T(8,128)(2,1)} %gather_fusion, bf16[256,128,128]{2,1,0:T(8,128)(2,1)} %get-tuple-element.274, s32[]{:T(128)S(6)} %select_n.44), kind=kOutput, calls=%fused_computation.4.clone.1 | convolution fusion | flops 538968064 | bytes 13631620 | tf_op jit(solution)/shard_map/while/body/tij,tjf->tif/dot_general | solution.py:46
  74.6 11.8 %scatter_fusion = f32[8,128,512]{2,1,0:T(8,128)S(1)} fusion(f32[8,128,512]{2,1,0:T(8,128)S(1)} %get-tuple-element.259, s32[32]{0:T(128)S(1)} %get-tuple-element.234, f32[32,128,512]{2,1,0:T(8,128)} %broadcast_multiply_fusion.5), kind=kCustom, calls=%fused_computation.2.clone.1 | custom fusion | flops 2097152 | bytes 25165952 | tf_op jit(solution)/shard_map/while/body/scatter-add | solution.py:49
  87.2 4.4 gather_fusion
  91.5 7.0 %broadcast_multiply_fusion.5 = f32[32,128,512]{2,1,0:T(8,128)} fusion(f32[32]{0:T(128)S(1)} %compare_convert_fusion.3, bf16[32,128,512]{2,1,0:T(8,128)(2,1)} %gather_fusion, bf16[256,128,128]{2,1,0:T(8,128)(2,1)} %get-tuple-element.274, s32[]{:T(128)S(6)} %select_n.44), kind=kOutput, calls=%fused_computation.4.clone.1 | convolution fusion | flops 538968064 | bytes 13631620 | tf_op jit(solution)/shard_map/while/body/tij,tjf->tif/dot_general | solution.py:46
  98.5 11.8 %scatter_fusion = f32[8,128,512]{2,1,0:T(8,128)S(1)} fusion(f32[8,128,512]{2,1,0:T(8,128)S(1)} %get-tuple-element.259, s32[32]{0:T(128)S(1)} %get-tuple-element.234, f32[32,128,512]{2,1,0:T(8,128)} %broadcast_multiply_fusion.5), kind=kCustom, calls=%fused_computation.2.clone.1 | custom fusion | flops 2097152 | bytes 25165952 | tf_op jit(solution)/shard_map/while/body/scatter-add | solution.py:49
  111.1 4.4 gather_fusion
  115.4 7.0 %broadcast_multiply_fusion.5 = f32[32,128,512]{2,1,0:T(8,128)} fusion(f32[32]{0:T(128)S(1)} %compare_convert_fusion.3, bf16[32,128,512]{2,1,0:T(8,128)(2,1)} %gather_fusion, bf16[256,128,128]{2,1,0:T(8,128)(2,1)} %get-tuple-element.274, s32[]{:T(128)S(6)} %select_n.44), kind=kOutput, calls=%fused_computation.4.clone.1 | convolution fusion | flops 538968064 | bytes 13631620 | tf_op jit(solution)/shard_map/while/body/tij,tjf->tif/dot_general | solution.py:46
  122.4 11.7 %scatter_fusion = f32[8,128,512]{2,1,0:T(8,128)S(1)} fusion(f32[8,128,512]{2,1,0:T(8,128)S(1)} %get-tuple-element.259, s32[32]{0:T(128)S(1)} %get-tuple-element.234, f32[32,128,512]{2,1,0:T(8,128)} %broadcast_multiply_fusion.5), kind=kCustom, calls=%fused_computation.2.clone.1 | custom fusion | flops 2097152 | bytes 25165952 | tf_op jit(solution)/shard_map/while/body/scatter-add | solution.py:49
  134.9 4.4 gather_fusion
  139.3 7.0 %broadcast_multiply_fusion.5 = f32[32,128,512]{2,1,0:T(8,128)} fusion(f32[32]{0:T(128)S(1)} %compare_convert_fusion.3, bf16[32,128,512]{2,1,0:T(8,128)(2,1)} %gather_fusion, bf16[256,128,128]{2,1,0:T(8,128)(2,1)} %get-tuple-element.274, s32[]{:T(128)S(6)} %select_n.44), kind=kOutput, calls=%fused_computation.4.clone.1 | convolution fusion | flops 538968064 | bytes 13631620 | tf_op jit(solution)/shard_map/while/body/tij,tjf->tif/dot_general | solution.py:46
  146.3 11.8 %scatter_fusion = f32[8,128,512]{2,1,0:T(8,128)S(1)} fusion(f32[8,128,512]{2,1,0:T(8,128)S(1)} %get-tuple-element.259, s32[32]{0:T(128)S(1)} %get-tuple-element.234, f32[32,128,512]{2,1,0:T(8,128)} %broadcast_multiply_fusion.5), kind=kCustom, calls=%fused_computation.2.clone.1 | custom fusion | flops 2097152 | bytes 25165952 | tf_op jit(solution)/shard_map/while/body/scatter-add | solution.py:49
  158.1 87.7 %all-reduce.7 = bf16[1024,512]{1,0:T(8,128)(2,1)} all-reduce(f32[1024,512]{1,0:T(8,128)S(1)} %bitcast.16), channel_id=1, replica_groups=mesh['node'=8,'rep'=4] {'rep'}, use_global_device_ids=true, to_apply=%region_3.4 | all-reduce | flops 524288 | bytes 3145728 | tf_op jit(solution)/shard_map/psum | solution.py:73
  245.8 5.3 fusion.6
  254.2 79.5 %all-reduce.4.cloned.1.call-done = f32[512,512]{1,0:T(8,128)} async-done(((f32[512,512]{1,0:T(8,128)}), f32[512,512]{1,0:T(8,128)}) %all-reduce.4.cloned.1.call-update) | async-done | bytes 1048592 | tf_op jit(solution)/shard_map/psum | solution.py:13
  336.3 117.3 %while.21 = (s32[]{:T(128)}, f32[16,128,512]{2,1,0:T(8,128)}, s32[]{:T(128)}, s32[256]{0:T(256)S(1)}, bf16[256,128,128]{2,1,0:T(8,128)(2,1)}, /*index=5*/s32[256...) while((s32[]{:T(128)}, f32[16,128,512]{2,1,0:T(8,128)}, ...), condition=%wide.region_8.9_spmd, body=%wide.region_6.8_spmd.sunk | while | flops 541066688 | bytes 47191480 | solution.py:51
  337.1 2.8 gather_fusion.1
  339.8 7.3 %broadcast_multiply_fusion.6 = f32[32,128,512]{2,1,0:T(8,128)} fusion(f32[32]{0:T(128)S(1)} %and_select_fusion.2, bf16[32,128,512]{2,1,0:T(8,128)(2,1)} %gather_fusion.1, bf16[256,128,128]{2,1,0:T(8,128)(2,1)} %get-tuple-element.310, s32[]{:T(128)S(6)} %select_n.46), kind=kOutput, calls=%fused_computation.11.clone.1 | convolution fusion | flops 538968064 | bytes 13631620 | tf_op jit(solution)/shard_map/while/body/tji,tjf->tif/dot_general | solution.py:42
  347.1 18.5 %scatter_fusion.1 = f32[16,128,512]{2,1,0:T(8,128)} fusion(f32[16,128,512]{2,1,0:T(8,128)} %get-tuple-element.295, s32[32]{0:T(128)S(1)} %get-tuple-element.244, f32[32,128,512]{2,1,0:T(8,128)} %broadcast_multiply_fusion.6), kind=kCustom, calls=%fused_computation.3.clone.1 | custom fusion | flops 2097152 | bytes 25165952 | tf_op jit(solution)/shard_map/while/body/scatter-add | solution.py:45
  366.4 2.8 gather_fusion.1
  369.2 7.3 %broadcast_multiply_fusion.6 = f32[32,128,512]{2,1,0:T(8,128)} fusion(f32[32]{0:T(128)S(1)} %and_select_fusion.2, bf16[32,128,512]{2,1,0:T(8,128)(2,1)} %gather_fusion.1, bf16[256,128,128]{2,1,0:T(8,128)(2,1)} %get-tuple-element.310, s32[]{:T(128)S(6)} %select_n.46), kind=kOutput, calls=%fused_computation.11.clone.1 | convolution fusion | flops 538968064 | bytes 13631620 | tf_op jit(solution)/shard_map/while/body/tji,tjf->tif/dot_general | solution.py:42
  376.5 18.6 %scatter_fusion.1 = f32[16,128,512]{2,1,0:T(8,128)} fusion(f32[16,128,512]{2,1,0:T(8,128)} %get-tuple-element.295, s32[32]{0:T(128)S(1)} %get-tuple-element.244, f32[32,128,512]{2,1,0:T(8,128)} %broadcast_multiply_fusion.6), kind=kCustom, calls=%fused_computation.3.clone.1 | custom fusion | flops 2097152 | bytes 25165952 | tf_op jit(solution)/shard_map/while/body/scatter-add | solution.py:45
  395.9 2.8 gather_fusion.1
  398.7 7.4 %broadcast_multiply_fusion.6 = f32[32,128,512]{2,1,0:T(8,128)} fusion(f32[32]{0:T(128)S(1)} %and_select_fusion.2, bf16[32,128,512]{2,1,0:T(8,128)(2,1)} %gather_fusion.1, bf16[256,128,128]{2,1,0:T(8,128)(2,1)} %get-tuple-element.310, s32[]{:T(128)S(6)} %select_n.46), kind=kOutput, calls=%fused_computation.11.clone.1 | convolution fusion | flops 538968064 | bytes 13631620 | tf_op jit(solution)/shard_map/while/body/tji,tjf->tif/dot_general | solution.py:42
  406.1 18.2 %scatter_fusion.1 = f32[16,128,512]{2,1,0:T(8,128)} fusion(f32[16,128,512]{2,1,0:T(8,128)} %get-tuple-element.295, s32[32]{0:T(128)S(1)} %get-tuple-element.244, f32[32,128,512]{2,1,0:T(8,128)} %broadcast_multiply_fusion.6), kind=kCustom, calls=%fused_computation.3.clone.1 | custom fusion | flops 2097152 | bytes 25165952 | tf_op jit(solution)/shard_map/while/body/scatter-add | solution.py:45
  425.1 2.8 gather_fusion.1
  427.9 7.3 %broadcast_multiply_fusion.6 = f32[32,128,512]{2,1,0:T(8,128)} fusion(f32[32]{0:T(128)S(1)} %and_select_fusion.2, bf16[32,128,512]{2,1,0:T(8,128)(2,1)} %gather_fusion.1, bf16[256,128,128]{2,1,0:T(8,128)(2,1)} %get-tuple-element.310, s32[]{:T(128)S(6)} %select_n.46), kind=kOutput, calls=%fused_computation.11.clone.1 | convolution fusion | flops 538968064 | bytes 13631620 | tf_op jit(solution)/shard_map/while/body/tji,tjf->tif/dot_general | solution.py:42
  435.2 18.5 %scatter_fusion.1 = f32[16,128,512]{2,1,0:T(8,128)} fusion(f32[16,128,512]{2,1,0:T(8,128)} %get-tuple-element.295, s32[32]{0:T(128)S(1)} %get-tuple-element.244, f32[32,128,512]{2,1,0:T(8,128)} %broadcast_multiply_fusion.6), kind=kCustom, calls=%fused_computation.3.clone.1 | custom fusion | flops 2097152 | bytes 25165952 | tf_op jit(solution)/shard_map/while/body/scatter-add | solution.py:45
  453.6 3.8 convert_element_type.37
  461.7 176.2 %reduce-scatter.2.cloned.1.call-done = bf16[256,512]{1,0:T(8,128)(2,1)} async-done(((bf16[2048,512]{1,0:T(8,128)(2,1)}), bf16[256,512]{1,0:T(8,128)(2,1)}) %reduce-scatter.2.cloned.1.call-update) | async-done | bytes 262160 | tf_op jit(solution)/shard_map/reduce_scatter | solution.py:89
  (48 shorter events, 17.8 us)
Async XLA Ops:
  7.2 238.7 %copy-start = (bf16[512,512]{1,0:T(8,128)(2,1)S(1)}, bf16[512,512]{1,0:T(8,128)(2,1)}, u32[]{:S(2)}) copy-start(bf16[512,512]{1,0:T(8,128)(2,1)} %param.12) | copy-start | bytes 1572868
  7.2 55.1 %copy-start.1 = (s32[256]{0:T(256)S(1)}, s32[256]{0:T(256)}, u32[]{:S(2)}) copy-start(s32[256]{0:T(256)} %param.16) | copy-start | bytes 3076
  7.2 55.1 %copy-start.2 = (s32[256]{0:T(256)S(1)}, s32[256]{0:T(256)}, u32[]{:S(2)}) copy-start(s32[256]{0:T(256)} %param.15) | copy-start | bytes 3076
  7.2 54.8 %all-gather.3.cloned.1.call-start = ((), (), s32[]{:S(2)}) async-start(), calls=%async_computation.1 | async-start | bytes 2359296 | tf_op jit(solution)/shard_map/all_gather | solution.py:60
  7.9 237.9 %all-gather.5.cloned.1.call-start = ((), (), s32[]{:S(2)}) async-start(), calls=%async_computation.2 | async-start | bytes 1310720 | tf_op jit(solution)/shard_map/all_gather | solution.py:74
  8.7 325.0 %all-reduce.4.cloned.1.call-start = ((), (), s32[]{:S(2)}) async-start(), calls=%async_computation.3 | async-start | bytes 2097152 | tf_op jit(solution)/shard_map/psum | solution.py:13
  253.4 206.0 %all-reduce.6.cloned.1.call-start = ((), (), s32[]{:S(2)}) async-start(), calls=%async_computation.4 | async-start | bytes 2097152 | tf_op jit(solution)/shard_map/psum | solution.py:13
  333.7 304.2 %reduce-scatter.2.cloned.1.call-start = ((), (), s32[]{:S(2)}) async-start(), calls=%async_computation.5 | async-start | bytes 2359296 | tf_op jit(solution)/shard_map/reduce_scatter | solution.py:89
Sparse Core Ops, SparseCore 0:
  10.1 51.7 all-gather.2
  63.5 15.2 all-gather.4
  253.6 80.1 all-reduce.3
  337.1 78.7 all-reduce.5
  457.6 180.3 reduce-scatter.1
